TPU v7x, 32 devices: a whole 2x2x4 slice. The times are simulated.
32 devices in a mesh: groups: 2 (over y), dp: 4 (over z), tensor: 4 (over x, core).
Axes of the slice: x: 2, y: 2, z: 4, core: 2. Of those that a mesh axis runs over, the one named last changes fastest.
Arguments:
- feature_cache: bfloat16 [512, 8, 3, 8192], P(('groups', 'dp'), None, None, 'tensor'), parts along dimension 0
- owner_ids: int32 [512, 1], P(('groups', 'dp')), parts along dimension 0, may hold values from 0 to 3; in each aligned block of 64 rows (0 to 63, 64 to 127, ...) at most 24 rows name the same one
- slot_ids: int32 [512], P(('groups', 'dp')), parts along dimension 0, may hold values from 0 to 63
- live_tokens: int32 [512], P(('groups', 'dp')), parts along dimension 0, may hold values from 1 to 8
- tap_gain: float32 [3, 8192], P(None, 'tensor'), may hold values from 0.1 to 1.9
- key_cotangent: bfloat16 [4096, 1024], P(('groups', 'dp'), 'tensor'), parts along dimension 0, may hold values from -0.1875 to 0.1875
- value_cotangent: bfloat16 [4096, 1024], P(('groups', 'dp'), 'tensor'), parts along dimension 0, may hold values from -0.1875 to 0.1875
Outputs:
- kv_gradient: float32 [4096, 8192], P(('groups', 'dp'), 'tensor'), parts along dimension 0
There are 2 independent parts, one for each index of `groups`. A program takes and returns all parts, laid end to end along the dimension named above; an argument that names none is the same for every part. Nothing has to cross between parts.
Inputs may be any that keep to these rules, and one draw needn't show every extreme that they name: `owner_ids`: among the 64 entries of one device's list, no owner is named more than 24 times, a bound that some block reaches.
All inputs are finite; a program needn't handle non-finite values.
Results may differ from a plain program's by a relative error of at most 0.009.
Values may be sent and summed in bfloat16 or wider, within the bound.
A program may use at most 128 MiB of HBM per device.

v0:
```python
import jax
import jax.numpy as jnp
from jax import lax
from jax.sharding import PartitionSpec as P

EPSILON = 1e-06


def united_of(feature_cache, tap_gain, width):
    floats = feature_cache.astype(jnp.float32)
    squares = lax.psum(jnp.sum(floats * floats, axis=-1), "tensor")
    inverse_rms = lax.rsqrt(squares / width + EPSILON)
    return jnp.sum(floats * inverse_rms[..., None] * tap_gain, axis=2).astype(jnp.bfloat16)


def slot_matrix(owner_ids, slot_ids, live_tokens, owned, dtype):
    index = owner_ids[:, 0] * owned + slot_ids
    table = lax.all_gather(jnp.stack([index, live_tokens]), "dp", axis=1, tiled=True)
    slots = lax.axis_size("dp") * owned
    chosen = jnp.arange(slots, dtype=jnp.int32)[:, None] == table[0][None, :]
    return (chosen.astype(dtype), table[1])


def body(feature_cache, owner_ids, slot_ids, live_tokens, tap_gain, key_cotangent, value_cotangent):
    owned, block_len, _, columns = feature_cache.shape
    width = columns * lax.axis_size("tensor")
    united = united_of(feature_cache, tap_gain, width).reshape(owned * block_len, columns)
    everywhere = lax.all_gather(united, "dp", axis=0, tiled=True)
    chosen, live = slot_matrix(owner_ids, slot_ids, live_tokens, owned, jnp.bfloat16)
    joined = jnp.concatenate(
        [
            lax.all_gather(key_cotangent, "tensor", axis=1, tiled=True),
            lax.all_gather(value_cotangent, "tensor", axis=1, tiled=True),
        ],
        axis=1,
    )
    mine = lax.all_to_all(joined, "dp", split_axis=1, concat_axis=0, tiled=True)
    rows = mine.shape[1]
    mine = mine.reshape(-1, block_len, rows)
    mask = jnp.arange(block_len, dtype=jnp.int32)[None, :] < live[:, None]
    mine = jnp.where(mask[:, :, None], mine, jnp.zeros_like(mine)).reshape(-1, block_len * rows)
    by_slot = (
        lax.dot_general(chosen, mine, (((1,), (0,)), ((), ())), preferred_element_type=jnp.float32)
        .astype(jnp.bfloat16)
        .reshape(-1, rows)
    )
    return lax.dot_general(
        by_slot, everywhere, (((0,), (0,)), ((), ())), preferred_element_type=jnp.float32
    )


def solution(mesh):
    in_specs = (
        P(("groups", "dp"), None, None, "tensor"),
        P(("groups", "dp"), None),
        P(("groups", "dp")),
        P(("groups", "dp")),
        P(None, "tensor"),
        P(("groups", "dp"), "tensor"),
        P(("groups", "dp"), "tensor"),
    )
    out_specs = P(("groups", "dp"), "tensor")
    return jax.shard_map(body, mesh=mesh, in_specs=in_specs, out_specs=out_specs, check_vma=False)
```

profile of v0, /device:TPU:0, one launch (start us, length us, event | category | flops | bytes accessed | tf_op | source)
XLA Modules:
  0.0 255.0 jit_solution(5300680193255701381)
XLA Ops:
  6.5 0.7 all-gather.5.cloned.1.call-update
  7.3 0.0 all-gather.7.cloned.1.call-start
  7.3 0.7 all-gather.7.cloned.1.call-update
  8.0 0.0 all-gather.9.cloned.1.call-start
  8.1 4.1 %fusion = f32[64,8,3]{1,2,0:T(4,128)S(1)} fusion(bf16[64,8,3,2048]{3,1,2,0:T(8,128)(2,1)} %param.7), kind=kLoop, calls=%fused_computation.2 | loop fusion | flops 9435648 | bytes 6297600 | tf_op jit(solution)/shard_map/reduce_sum | solution.py:11
  12.2 0.1 copy.17
  12.3 13.1 %psum.7 = f32[64,8,3]{0,1,2:T(8,128)S(1)} all-reduce(f32[64,8,3]{0,1,2:T(8,128)S(1)} %copy.17), channel_id=1, replica_groups=mesh['groups'=2,'dp'=4,'tensor'=4] {'tensor'}, use_global_device_ids=true, to_apply=%region_1.0 | all-reduce | flops 1536 | bytes 12288 | tf_op jit(solution)/shard_map/psum | solution.py:11
  25.4 0.1 copy.18
  25.5 6.9 %fusion.2 = bf16[64,8,2048]{2,1,0:T(8,128)(2,1)} fusion(bf16[64,8,3,2048]{3,1,2,0:T(8,128)(2,1)} %param.7, f32[3,2048]{1,0:T(4,128)S(1)} %copy-done, f32[64,8,3]{1,2,0:T(4,128)S(1)} %copy.18), kind=kLoop, calls=%fused_computation.4 | loop fusion | flops 11534336 | bytes 8419328 | tf_op jit(solution)/shard_map/reduce_sum | solution.py:13
  32.5 14.6 %all-gather.7.cloned.1.call-done = bf16[512,1024]{1,0:T(8,128)(2,1)} async-done(((bf16[512,256]{1,0:T(8,128)(2,1)}), bf16[512,1024]{1,0:T(8,128)(2,1)}) %all-gather.7.cloned.1.call-update) | async-done | bytes 1048592 | tf_op jit(solution)/shard_map/all_gather | solution.py:33
  47.0 1.7 pad_maximum_fusion
  48.8 1.5 copy.22
  50.3 4.6 %all-to-all-start = ((bf16[512,4,512]{2,0,1:T(8,128)(2,1)}), bf16[512,4,512]{2,0,1:T(8,128)(2,1)S(1)}, u32[]{:S(2)}, u32[]{:S(2)}) async-start(bf16[512,4,512]{2,0,1:T(8,128)(2,1)} %bitcast.29), calls=%async_computation | async-start | bytes 4194304 | tf_op jit(solution)/shard_map/all_to_all | solution.py:37
  55.0 71.3 %all-gather = s32[4,64,2]{1,2,0:T(2,128)S(1)} all-gather(s32[1,64,2]{1,2,0:T(2,128)S(1)} %add_bitcast_fusion), channel_id=1, replica_groups=mesh['groups'=2,'dp'=4,'tensor'=4] {'dp'}, dimensions={0}, use_global_device_ids=true | all-gather | bytes 2560 | tf_op jit(solution)/shard_map/all_gather | solution.py:18
  126.3 0.1 reshape.47
  126.4 0.1 iota_compare_fusion.2
  126.5 0.5 broadcast_in_dim.18
  126.9 0.8 copy.20
  127.7 32.2 %all-to-all-done = bf16[512,4,512]{2,0,1:T(8,128)(2,1)S(1)} async-done(((bf16[512,4,512]{2,0,1:T(8,128)(2,1)}), bf16[512,4,512]{2,0,1:T(8,128)(2,1)S(1)}, u32[]{:S(2)}, u32[]{:S(2)}) %all-to-all-start) | async-done | bytes 2097184 | tf_op jit(solution)/shard_map/all_to_all | solution.py:37
  159.9 2.3 reshape.44
  162.3 3.7 %convolution_convert_fusion = bf16[256,4096]{1,0:T(8,128)(2,1)} fusion(pred[256,4096]{1,0:T(8,128)(4,1)S(1)} %bitcast.33, bf16[256,4096]{1,0:T(8,128)(2,1)} %reshape.44, s32[256]{0:T(256)S(1)} %bitcast.36), kind=kOutput, calls=%fused_computation.5 | convolution fusion | flops 539033600 | bytes 5243904 | tf_op jit(solution)/shard_map/dot_general | solution.py:43
  165.9 2.9 %reshape.45 = bf16[2048,512]{1,0:T(8,128)(2,1)S(1)} reshape(bf16[256,4096]{1,0:T(8,128)(2,1)} %convolution_convert_fusion) | data formatting | bytes 4194304 | tf_op jit(solution)/shard_map/reshape | solution.py:45
  168.8 70.2 %all-gather.9.cloned.1.call-done = bf16[2048,2048]{1,0:T(8,128)(2,1)} async-done(((bf16[512,2048]{1,0:T(8,128)(2,1)}), bf16[2048,2048]{1,0:T(8,128)(2,1)}) %all-gather.9.cloned.1.call-update) | async-done | bytes 8388624 | tf_op jit(solution)/shard_map/all_gather | solution.py:28
  239.0 9.4 %fusion.9 = f32[512,2048]{1,0:T(8,128)} fusion(bf16[2048,512]{1,0:T(8,128)(2,1)S(1)} %reshape.45, bf16[2048,2048]{1,0:T(8,128)(2,1)} %all-gather.9.cloned.1.call-done), kind=kOutput, calls=%fused_computation.20 | convolution fusion | flops 4294967296 | bytes 14680064 | tf_op jit(solution)/shard_map/dot_general | solution.py:47
  (16 shorter events, 0.1 us)
Async XLA Ops:
  6.5 19.0 %copy-start = (f32[3,2048]{1,0:T(4,128)S(1)}, f32[3,2048]{1,0:T(4,128)}, u32[]{:S(2)}) copy-start(f32[3,2048]{1,0:T(4,128)} %param.11) | copy-start | bytes 73732
  6.5 25.9 %all-gather.5.cloned.1.call-start = ((), (), s32[]{:S(2)}) async-start(), calls=%async_computation.1 | async-start | bytes 1310720 | tf_op jit(solution)/shard_map/all_gather | solution.py:32
  7.3 39.8 %all-gather.7.cloned.1.call-start = ((), (), s32[]{:S(2)}) async-start(), calls=%async_computation.2 | async-start | bytes 1310720 | tf_op jit(solution)/shard_map/all_gather | solution.py:33
  8.0 231.0 %all-gather.9.cloned.1.call-start = ((), (), s32[]{:S(2)}) async-start(), calls=%async_computation.3 | async-start | bytes 10485760 | tf_op jit(solution)/shard_map/all_gather | solution.py:28
  48.8 6.1 %copy-start.2 = (s32[64]{0:T(128)S(1)}, s32[64]{0:T(128)}, u32[]{:S(2)}) copy-start(s32[64]{0:T(128)} %param.9) | copy-start | bytes 772
  48.8 6.1 %copy-start.3 = (s32[64,1]{0,1:T(1,128)S(1)}, s32[64,1]{0,1:T(1,128)}, u32[]{:S(2)}) copy-start(s32[64,1]{0,1:T(1,128)} %param.8) | copy-start | bytes 772
  48.8 6.1 %copy-start.1 = (s32[64]{0:T(128)S(1)}, s32[64]{0:T(128)}, u32[]{:S(2)}) copy-start(s32[64]{0:T(128)} %param.10) | copy-start | bytes 772
  50.3 109.6 %all-to-all-start = ((bf16[512,4,512]{2,0,1:T(8,128)(2,1)}), bf16[512,4,512]{2,0,1:T(8,128)(2,1)S(1)}, u32[]{:S(2)}, u32[]{:S(2)}) async-start(bf16[512,4,512]{2,0,1:T(8,128)(2,1)} %bitcast.29), calls=%async_computation | async-start | bytes 4194304 | tf_op jit(solution)/shard_map/all_to_all | solution.py:37
Sparse Core Ops, SparseCore 0:
  8.9 19.6 all-gather.4
  30.2 16.8 all-gather.6
  48.6 190.3 all-gather.8
where the time goes:
time: 255 us
  waiting for transfers between devices  118 us (46%)
  blocking collectives  84.5 us (33%)
  between operations  13.2 us (5%)
  matrix products  13.1 us (5%)
  other arithmetic  12.9 us (5%)
  local copies, waits for them, and re-layouts  8.19 us (3%)
  starting transfers between devices  4.68 us (2%)
    all_gather x1, blocking collectives, slot_matrix(): lax.all_gather(jnp.stack([index, live_tokens]), 'dp', axis=1, tiled=True)  71.3 us
    all_gather x1, waiting for transfers between devices, body(): everywhere = lax.all_gather(united, 'dp', axis=0, tiled=True)  70.2 us
    all_to_all x1, waiting for transfers between devices, body(): mine = lax.all_to_all(joined, 'dp', split_axis=1, concat_axis=0, tiled=True)  32.2 us
    all_gather x1, waiting for transfers between devices, body(): lax.all_gather(value_cotangent, 'tensor', axis=1, tiled=True)  14.6 us
    psum x1, blocking collectives, united_of(): squares = lax.psum(jnp.sum(floats * floats, axis=-1), 'tensor')  13.1 us
    dot_general x1, matrix products, body(): lax.dot_general(by_slot, everywhere, (((0,), (0,)), ((), ())), preferred_...  9.44 us
    reduce_sum x1, other arithmetic, united_of(): jnp.sum(floats * inverse_rms[..., None] * tap_gain, axis=2)  6.9 us
  transfers between devices with their start and end apart: 4, of which 3 were waited for; matrix products, arithmetic and copies ran while one was open for 10% of the time, Pallas kernels for 0%

commit v1 on v0

--- a/solution.py
+++ b/solution.py
@@ -4,6 +4,18 @@
 from jax.sharding import PartitionSpec as P
 
 EPSILON = 1e-06
+
+
+def doubled_up(x, axis, dim):
+    ways, here = (lax.axis_size(axis), lax.axis_index(axis))
+    grown, reach = (x, 1)
+    while reach < ways:
+        theirs = lax.ppermute(grown, axis, [(d, d ^ reach) for d in range(ways)])
+        mine_first = jnp.concatenate([grown, theirs], axis=dim)
+        theirs_first = jnp.concatenate([theirs, grown], axis=dim)
+        grown = jnp.where(here & reach == 0, mine_first, theirs_first)
+        reach = 2 * reach
+    return grown
 
 
 def united_of(feature_cache, tap_gain, width):
@@ -30,7 +42,7 @@
     joined = jnp.concatenate(
         [
             lax.all_gather(key_cotangent, "tensor", axis=1, tiled=True),
-            lax.all_gather(value_cotangent, "tensor", axis=1, tiled=True),
+            doubled_up(value_cotangent, "tensor", 1),
         ],
         axis=1,
     )

time: 255 us -> 243 us (0.953)
  waiting for transfers between devices: 118 us -> 101 us
  blocking collectives: 84.5 us -> 87.1 us
    ppermute x0 -> x2, waiting for transfers between devices: none -> 15.1 us  [doubled_up(): theirs = lax.ppermute(grown, axis, [(d, d ^ reach) for d in range(ways)])]
    all_gather x1 -> x0, waiting for transfers between devices: 14.6 us -> none  [body(): lax.all_gather(value_cotangent, 'tensor', axis=1, tiled=True)]
    all_gather x1, waiting for transfers between devices: 70.2 us -> 58.7 us  [body(): everywhere = lax.all_gather(united, 'dp', axis=0, tiled=True)]
    all_to_all x1, waiting for transfers between devices: 32.2 us -> 27 us  [body(): mine = lax.all_to_all(joined, 'dp', split_axis=1, concat_axis=0, tiled=True)]
    all_gather x1, blocking collectives: 71.3 us -> 74 us  [slot_matrix(): lax.all_gather(jnp.stack([index, live_tokens]), 'dp', axis=1, tiled=True)]
  transfers between devices with their start and end apart: 4 -> 5, of which waited for: 3 -> 4; matrix products, arithmetic and copies ran while one was open for 10% -> 10% of each run, Pallas kernels for 0% -> 0%
where the time goes in v1:
time: 243 us
  waiting for transfers between devices  101 us (42%)
  blocking collectives  87.1 us (36%)
  between operations  13.5 us (6%)
  matrix products  13.1 us (5%)
  other arithmetic  12.9 us (5%)
  local copies, waits for them, and re-layouts  9.11 us (4%)
  starting transfers between devices  5.49 us (2%)
    all_gather x1, blocking collectives, slot_matrix(): lax.all_gather(jnp.stack([index, live_tokens]), 'dp', axis=1, tiled=True)  74 us
    all_gather x1, waiting for transfers between devices, body(): everywhere = lax.all_gather(united, 'dp', axis=0, tiled=True)  58.7 us
    all_to_all x1, waiting for transfers between devices, body(): mine = lax.all_to_all(joined, 'dp', split_axis=1, concat_axis=0, tiled=True)  27 us
    ppermute x2, waiting for transfers between devices, doubled_up(): theirs = lax.ppermute(grown, axis, [(d, d ^ reach) for d in range(ways)])  15.1 us
    psum x1, blocking collectives, united_of(): squares = lax.psum(jnp.sum(floats * floats, axis=-1), 'tensor')  13.1 us
    dot_general x1, matrix products, body(): lax.dot_general(by_slot, everywhere, (((0,), (0,)), ((), ())), preferred_...  9.44 us
    reduce_sum x1, other arithmetic, united_of(): jnp.sum(floats * inverse_rms[..., None] * tap_gain, axis=2)  6.86 us
    all_to_all x1, starting transfers between devices, body(): mine = lax.all_to_all(joined, 'dp', split_axis=1, concat_axis=0, tiled=True)  4.97 us
  transfers between devices with their start and end apart: 5, of which 4 were waited for; matrix products, arithmetic and copies ran while one was open for 10% of the time, Pallas kernels for 0%

profile of v1, /device:TPU:0, one launch (start us, length us, event | category | flops | bytes accessed | tf_op | source)
XLA Modules:
  0.0 242.8 jit_solution(5431102361711027277)
XLA Ops:
  6.5 0.7 all-gather.4.cloned.1.call-update
  7.3 4.1 %fusion = f32[64,8,3]{1,2,0:T(4,128)S(1)} fusion(bf16[64,8,3,2048]{3,1,2,0:T(8,128)(2,1)} %param.7), kind=kLoop, calls=%fused_computation.2 | loop fusion | flops 9435648 | bytes 6297600 | tf_op jit(solution)/shard_map/reduce_sum | solution.py:23
  11.5 13.1 %psum.7 = f32[64,8,3]{0,1,2:T(8,128)S(1)} all-reduce(f32[64,8,3]{0,1,2:T(8,128)S(1)} %copy.17), channel_id=1, replica_groups=mesh['groups'=2,'dp'=4,'tensor'=4] {'tensor'}, use_global_device_ids=true, to_apply=%region_1.0 | all-reduce | flops 1536 | bytes 12288 | tf_op jit(solution)/shard_map/psum | solution.py:23
  24.6 0.1 copy.18
  24.8 6.9 %fusion.2 = bf16[64,8,2048]{2,1,0:T(8,128)(2,1)} fusion(bf16[64,8,3,2048]{3,1,2,0:T(8,128)(2,1)} %param.7, f32[3,2048]{1,0:T(4,128)S(1)} %copy-done.1, f32[64,8,3]{1,2,0:T(4,128)S(1)} %copy.18), kind=kLoop, calls=%fused_computation.4 | loop fusion | flops 11534336 | bytes 8419328 | tf_op jit(solution)/shard_map/reduce_sum | solution.py:25
  31.7 0.9 copy-done
  32.6 1.5 collective-permute-done
  34.1 0.1 maximum_select_fusion.1
  34.2 0.5 collective-permute-start.1
  34.7 13.6 %collective-permute-done.1 = bf16[512,512]{1,0:T(8,128)(2,1)S(1)} collective-permute-done((bf16[512,512]{1,0:T(8,128)(2,1)S(1)}, bf16[512,512]{1,0:T(8,128)(2,1)S(1)}, u32[]{:S(2)}, u32[]{:S(2)}) %collective-permute-start.1) | collective-permute-done | bytes 524320 | tf_op jit(solution)/shard_map/ppermute | solution.py:13
  48.3 0.3 maximum_select_fusion
  48.6 1.4 pad_maximum_fusion
  50.0 1.5 copy.22
  51.5 5.0 %all-to-all-start = ((bf16[512,4,512]{2,0,1:T(8,128)(2,1)}), bf16[512,4,512]{2,0,1:T(8,128)(2,1)S(1)}, u32[]{:S(2)}, u32[]{:S(2)}) async-start(bf16[512,4,512]{2,0,1:T(8,128)(2,1)} %bitcast.29), calls=%async_computation | async-start | bytes 4194304 | tf_op jit(solution)/shard_map/all_to_all | solution.py:49
  56.5 74.0 %all-gather = s32[4,64,2]{1,2,0:T(2,128)S(1)} all-gather(s32[1,64,2]{1,2,0:T(2,128)S(1)} %add_bitcast_fusion), channel_id=1, replica_groups=mesh['groups'=2,'dp'=4,'tensor'=4] {'dp'}, dimensions={0}, use_global_device_ids=true | all-gather | bytes 2560 | tf_op jit(solution)/shard_map/all_gather | solution.py:30
  130.6 0.1 iota_compare_fusion.2
  130.7 0.5 broadcast_in_dim.18
  131.2 0.8 copy.20
  131.9 27.0 %all-to-all-done = bf16[512,4,512]{2,0,1:T(8,128)(2,1)S(1)} async-done(((bf16[512,4,512]{2,0,1:T(8,128)(2,1)}), bf16[512,4,512]{2,0,1:T(8,128)(2,1)S(1)}, u32[]{:S(2)}, u32[]{:S(2)}) %all-to-all-start) | async-done | bytes 2097184 | tf_op jit(solution)/shard_map/all_to_all | solution.py:49
  158.9 2.3 reshape.44
  161.2 3.7 %convolution_convert_fusion = bf16[256,4096]{1,0:T(8,128)(2,1)} fusion(pred[256,4096]{1,0:T(8,128)(4,1)S(1)} %bitcast.33, bf16[256,4096]{1,0:T(8,128)(2,1)} %reshape.44, s32[256]{0:T(256)S(1)} %bitcast.36), kind=kOutput, calls=%fused_computation.5 | convolution fusion | flops 539033600 | bytes 5243904 | tf_op jit(solution)/shard_map/dot_general | solution.py:55
  164.9 2.9 %reshape.45 = bf16[2048,512]{1,0:T(8,128)(2,1)S(1)} reshape(bf16[256,4096]{1,0:T(8,128)(2,1)} %convolution_convert_fusion) | data formatting | bytes 4194304 | tf_op jit(solution)/shard_map/reshape | solution.py:57
  167.8 58.7 %all-gather.6.cloned.1.call-done = bf16[2048,2048]{1,0:T(8,128)(2,1)} async-done(((bf16[512,2048]{1,0:T(8,128)(2,1)}), bf16[2048,2048]{1,0:T(8,128)(2,1)}) %all-gather.6.cloned.1.call-update) | async-done | bytes 8388624 | tf_op jit(solution)/shard_map/all_gather | solution.py:40
  226.5 9.4 %fusion.9 = f32[512,2048]{1,0:T(8,128)} fusion(bf16[2048,512]{1,0:T(8,128)(2,1)S(1)} %reshape.45, bf16[2048,2048]{1,0:T(8,128)(2,1)} %all-gather.6.cloned.1.call-done), kind=kOutput, calls=%fused_computation.22 | convolution fusion | flops 4294967296 | bytes 14680064 | tf_op jit(solution)/shard_map/dot_general | solution.py:59
  (21 shorter events, 0.3 us)
Async XLA Ops:
  6.5 42.1 %all-gather.4.cloned.1.call-start = ((), (), s32[]{:S(2)}) async-start(), calls=%async_computation.1 | async-start | bytes 1310720 | tf_op jit(solution)/shard_map/all_gather | solution.py:44
  7.3 17.5 %copy-start.1 = (f32[3,2048]{1,0:T(4,128)S(1)}, f32[3,2048]{1,0:T(4,128)}, u32[]{:S(2)}) copy-start(f32[3,2048]{1,0:T(4,128)} %param.11) | copy-start | bytes 73732
  7.3 219.2 %all-gather.6.cloned.1.call-start = ((), (), s32[]{:S(2)}) async-start(), calls=%async_computation.2 | async-start | bytes 10485760 | tf_op jit(solution)/shard_map/all_gather | solution.py:40
  31.6 0.9 copy-start
  32.6 1.5 collective-permute-start
  34.2 14.0 %collective-permute-start.1 = (bf16[512,512]{1,0:T(8,128)(2,1)S(1)}, bf16[512,512]{1,0:T(8,128)(2,1)S(1)}, u32[]{:S(2)}, u32[]{:S(2)}) collective-permute-start(bf16[512,512]{1,0:T(8,128)(2,1)S(1)} %maximum_select_fusion.1), channel_id=1, source_target_pairs={{0,2},{1,3},{2,0},{3,1},{4,6},{5,7},{6,4},{7,5},{8,10},{9,11},{10,... | collective-permute-start | bytes 1572872 | tf_op jit(solution)/shard_map/ppermute | solution.py:13
  51.5 5.0 %copy-start.3 = (s32[64]{0:T(128)S(1)}, s32[64]{0:T(128)}, u32[]{:S(2)}) copy-start(s32[64]{0:T(128)} %param.9) | copy-start | bytes 772
  51.5 5.0 %copy-start.4 = (s32[64,1]{0,1:T(1,128)S(1)}, s32[64,1]{0,1:T(1,128)}, u32[]{:S(2)}) copy-start(s32[64,1]{0,1:T(1,128)} %param.8) | copy-start | bytes 772
  51.5 5.0 %copy-start.2 = (s32[64]{0:T(128)S(1)}, s32[64]{0:T(128)}, u32[]{:S(2)}) copy-start(s32[64]{0:T(128)} %param.10) | copy-start | bytes 772
  51.5 107.4 %all-to-all-start = ((bf16[512,4,512]{2,0,1:T(8,128)(2,1)}), bf16[512,4,512]{2,0,1:T(8,128)(2,1)S(1)}, u32[]{:S(2)}, u32[]{:S(2)}) async-start(bf16[512,4,512]{2,0,1:T(8,128)(2,1)} %bitcast.29), calls=%async_computation | async-start | bytes 4194304 | tf_op jit(solution)/shard_map/all_to_all | solution.py:49
Sparse Core Ops, SparseCore 0:
  8.9 19.6 all-gather.3
  31.8 194.6 all-gather.5
